TPU v7x, 32 devices: a whole 2x2x4 slice. The times are simulated.
32 devices in a mesh: ctx: 8 (over y, x, core), fsdp: 4 (over z).
Axes of the slice: x: 2, y: 2, z: 4, core: 2. Of those that a mesh axis runs over, the one named last changes fastest.
Arguments:
- tokens: bfloat16 [4, 4096, 2048], P('fsdp', 'ctx'), may hold values from -6 to 6
- cotangent: bfloat16 [4, 4096, 2048], P('fsdp', 'ctx'), may hold values from -6 to 6
- kv_cotangent: bfloat16 [4, 4096, 256], P('fsdp', 'ctx'), may hold values from -6 to 6
- lengths: int32 [4], P('fsdp'), may hold values from 1024 to 4096, as said below
- block_order: int32 [4, 16], P('fsdp'), may hold values from 0 to 15, each once within a row
- w_query: bfloat16 [2048, 2048], P('fsdp'), may hold values from -0.125 to 0.125
- w_kv: bfloat16 [2048, 256], P('fsdp'), may hold values from -0.25 to 0.25
- w_out: bfloat16 [2048, 2048], P('fsdp'), may hold values from -0.375 to 0.375
- gain_attn: bfloat16 [2048], P('fsdp'), may hold values from 0.5 to 1.5
- gain_ffn: bfloat16 [2048], P('fsdp'), may hold values from 0.5 to 1.5
- w_gate: bfloat16 [2048, 5632], P(None, 'fsdp'), may hold values from -0.125 to 0.125
- w_up: bfloat16 [2048, 5632], P(None, 'fsdp'), may hold values from -0.125 to 0.125
- w_down: bfloat16 [2048, 5632], P(None, 'fsdp'), may hold values from -0.078125 to 0.078125
Outputs:
- output: bfloat16 [4, 4096, 2048], P('fsdp', 'ctx')
- input_grad: bfloat16 [4, 4096, 2048], P('fsdp', 'ctx')
- grad_w_query: float32 [2048, 2048], P(('ctx', 'fsdp'))
- grad_w_kv: float32 [2048, 256], P(('ctx', 'fsdp'))
- grad_w_out: float32 [2048, 2048], P(('ctx', 'fsdp'))
- grad_gain_attn: float32 [2048], P(('ctx', 'fsdp'))
- grad_gain_ffn: float32 [2048], P(('ctx', 'fsdp'))
- grad_w_gate: float32 [2048, 5632], P('ctx', 'fsdp')
- grad_w_up: float32 [2048, 5632], P('ctx', 'fsdp')
- grad_w_down: float32 [2048, 5632], P('ctx', 'fsdp')
Inputs may be any that keep to these rules, and one draw needn't show every extreme that they name: Slot s holds one sequence of lengths[s] tokens; in every draw some slot is full. Each row is a permutation: stored block j of slot s, its tokens j * 256 to (j + 1) * 256 - 1, holds positions block_order[s, j] * 256 onward.
All inputs are finite; a program needn't handle non-finite values.
Results may differ from a plain program's by a relative error of at most 0.025.
Values may be sent and summed in bfloat16 or wider, within the bound.
No kernel may reach another device: no remote copies, remote signals or barrier semaphores. Data moves between devices by JAX's collectives and lax.ppermute only.
A program may use at most 448 MiB of HBM per device.

v0:
```python
import jax
import jax.numpy as jnp
from jax import lax
from jax.sharding import PartitionSpec as P

H = 16
HD = 128
EPSILON = 1e-05
ROPE_BASE = 10000.0
MASKED = -1e30


def angles(positions, head_dim):
    half_dim = head_dim // 2
    frequency = ROPE_BASE ** (-2.0 * jnp.arange(half_dim, dtype=jnp.float32) / head_dim)
    phase_angle = positions.astype(jnp.float32)[:, None] * frequency[None, :]
    return (jnp.cos(phase_angle), jnp.sin(phase_angle))


def rotate(vectors, cosine, sine_vals):
    half_dim = cosine.shape[-1]
    first_half = vectors[..., :half_dim]
    second_half = vectors[..., half_dim:]
    return jnp.concatenate(
        [
            first_half * cosine - second_half * sine_vals,
            second_half * cosine + first_half * sine_vals,
        ],
        axis=-1,
    )


def contract_rows(left, right):
    return lax.dot_general(
        left, right, (((0,), (0,)), ((), ())), preferred_element_type=jnp.float32
    )


def contract_cols(left, right):
    return lax.dot_general(
        left, right, (((1,), (1,)), ((), ())), preferred_element_type=jnp.float32
    )


def score_block(query_rows, row_pos, keys_all, key_pos, length, offset_at, block_width):
    key_part = lax.dynamic_slice_in_dim(keys_all, offset_at, block_width, 0)
    pos_part = lax.dynamic_slice_in_dim(key_pos, offset_at, block_width, 0)
    scores = contract_cols(query_rows, key_part)
    allowed = (pos_part[None, :] <= row_pos[:, None]) & (pos_part[None, :] < length)
    return jnp.where(allowed, scores, MASKED)


def attention_forward(query_rot, kv_slot, query_pos, key_pos, length):
    local_len, head_count, head_dim = query_rot.shape
    rows_total = local_len * head_count
    query_rows = query_rot.reshape(rows_total, head_dim)
    row_pos = jnp.repeat(query_pos, head_count)
    keys_all = kv_slot[:, :head_dim]
    values_all = kv_slot[:, head_dim:]
    block_width = min(512, kv_slot.shape[0])
    steps_count = kv_slot.shape[0] // block_width

    def stat_update(carried, offset_at):
        maximum, running_sum = carried
        scores = score_block(query_rows, row_pos, keys_all, key_pos, length, offset_at, block_width)
        new_max = jnp.maximum(maximum, jnp.max(scores, axis=1))
        summed = running_sum * jnp.exp(maximum - new_max) + jnp.sum(
            jnp.exp(scores - new_max[:, None]), axis=1
        )
        return (new_max, summed)

    def stat_step(carried, step_index):
        offset_at = step_index * block_width
        carried = stat_update(carried, offset_at)
        return (carried, None)

    initial = (jnp.full((rows_total,), MASKED, jnp.float32), jnp.zeros((rows_total,), jnp.float32))
    (maximum, running_sum), unused = lax.scan(
        stat_step, initial, jnp.arange(steps_count, dtype=jnp.int32)
    )
    log_total = maximum + jnp.log(running_sum)

    def value_update(accumulated, offset_at):
        scores = score_block(query_rows, row_pos, keys_all, key_pos, length, offset_at, block_width)
        weights_low = jnp.exp(scores - log_total[:, None]).astype(jnp.bfloat16)
        value_part = lax.dynamic_slice_in_dim(values_all, offset_at, block_width, 0)
        return accumulated + jnp.dot(weights_low, value_part, preferred_element_type=jnp.float32)

    def value_step(accumulated, step_index):
        offset_at = step_index * block_width
        accumulated = value_update(accumulated, offset_at)
        return (accumulated, None)

    attention, unused = lax.scan(
        value_step,
        jnp.zeros((rows_total, head_dim), jnp.float32),
        jnp.arange(steps_count, dtype=jnp.int32),
    )
    return (attention.reshape(local_len, head_count * head_dim), log_total)


def attention_backward(
    query_rot, kv_slot, query_pos, key_pos, length, log_total, grad_attn, row_delta
):
    local_len, head_count, head_dim = query_rot.shape
    rows_total = local_len * head_count
    query_rows = query_rot.reshape(rows_total, head_dim)
    grad_rows = grad_attn.reshape(rows_total, head_dim)
    row_pos = jnp.repeat(query_pos, head_count)
    keys_all = kv_slot[:, :head_dim]
    values_all = kv_slot[:, head_dim:]
    block_width = min(512, kv_slot.shape[0])
    steps_count = kv_slot.shape[0] // block_width

    def grad_update(grad_query, offset_at):
        scores = score_block(query_rows, row_pos, keys_all, key_pos, length, offset_at, block_width)
        probability = jnp.exp(scores - log_total[:, None])
        key_part = lax.dynamic_slice_in_dim(keys_all, offset_at, block_width, 0)
        value_part = lax.dynamic_slice_in_dim(values_all, offset_at, block_width, 0)
        grad_prob = contract_cols(grad_rows, value_part)
        grad_score = (probability * (grad_prob - row_delta[:, None])).astype(jnp.bfloat16)
        grad_key = contract_rows(grad_score, query_rows)
        grad_value = contract_rows(probability.astype(jnp.bfloat16), grad_rows)
        updated = grad_query + jnp.dot(grad_score, key_part, preferred_element_type=jnp.float32)
        return (updated, jnp.concatenate([grad_key, grad_value], axis=1))

    def grad_step(grad_query, step_index):
        offset_at = step_index * block_width
        return grad_update(grad_query, offset_at)

    grad_query, key_grads = lax.scan(
        grad_step,
        jnp.zeros((rows_total, head_dim), jnp.float32),
        jnp.arange(steps_count, dtype=jnp.int32),
    )
    return (
        grad_query.reshape(local_len, head_count, head_dim),
        key_grads.reshape(steps_count * block_width, 2 * head_dim),
    )


def swiglu_back(gate_proj, up_proj, grad_hidden):
    sigmoid_gate = jax.nn.sigmoid(gate_proj)
    grad_float = grad_hidden.astype(jnp.float32)
    grad_gate = (
        grad_float * up_proj * sigmoid_gate * (1.0 + gate_proj * (1.0 - sigmoid_gate))
    ).astype(jnp.bfloat16)
    grad_up = (grad_float * (gate_proj * sigmoid_gate)).astype(jnp.bfloat16)
    return (grad_gate, grad_up)


def split_term(left, right, ctx_count, fsdp_count):
    left_split = left.reshape(left.shape[0], ctx_count, left.shape[1] // ctx_count)
    right_split = right.reshape(right.shape[0], fsdp_count, right.shape[1] // fsdp_count)
    grad_term = jnp.einsum(
        "tcd,tfk->cfdk", left_split, right_split, preferred_element_type=jnp.float32
    )
    return grad_term.reshape(ctx_count * fsdp_count * grad_term.shape[2], grad_term.shape[3])


def shards(
    tokens,
    cotangent,
    kv_cotangent,
    lengths,
    block_order,
    w_query,
    w_kv,
    w_out,
    gain_attn,
    gain_ffn,
    w_gate,
    w_up,
    w_down,
):
    slots_here, local_len, model_dim = tokens.shape
    ctx_count = lax.axis_size("ctx")
    fsdp_count = lax.axis_size("fsdp")
    head_dim = HD
    head_count = H
    block_len = local_len // 2
    slot_len = local_len * ctx_count
    local_rows = slots_here * local_len
    offsets = jnp.arange(slot_len, dtype=jnp.int32) % block_len
    key_pos = jnp.repeat(block_order, block_len, axis=1) * block_len + offsets[None, :]
    query_pos = lax.dynamic_slice_in_dim(key_pos, lax.axis_index("ctx") * local_len, local_len, 1)
    live_rows = (query_pos < lengths[:, None]).reshape(local_rows, 1)
    query_full, kv_full, out_full, gain_one, gain_two = (
        lax.all_gather(w_query, "fsdp", axis=0, tiled=True),
        lax.all_gather(w_kv, "fsdp", axis=0, tiled=True),
        lax.all_gather(w_out, "fsdp", axis=0, tiled=True),
        lax.all_gather(gain_attn, "fsdp", axis=0, tiled=True),
        lax.all_gather(gain_ffn, "fsdp", axis=0, tiled=True),
    )
    tokens_flat = tokens.reshape(local_rows, model_dim).astype(jnp.float32)
    inverse_one = lax.rsqrt(jnp.mean(tokens_flat * tokens_flat, axis=1, keepdims=True) + EPSILON)
    unit_one = tokens_flat * inverse_one
    normed_attn = (unit_one * gain_one.astype(jnp.float32)).astype(jnp.bfloat16)
    queries = jnp.dot(normed_attn, query_full, preferred_element_type=jnp.float32).reshape(
        local_rows, head_count, head_dim
    )
    key_value = jnp.dot(normed_attn, kv_full, preferred_element_type=jnp.float32)
    cosine, sine_vals = angles(query_pos.reshape(local_rows), head_dim)
    query_rot = (
        rotate(queries, cosine[:, None, :], sine_vals[:, None, :]) * head_dim ** (-0.5)
    ).astype(jnp.bfloat16)
    key_rot = rotate(key_value[:, :head_dim], cosine, sine_vals).astype(jnp.bfloat16)
    local_kv = jnp.concatenate([key_rot, key_value[:, head_dim:].astype(jnp.bfloat16)], axis=1)
    slot_kv = lax.all_gather(
        local_kv.reshape(slots_here, local_len, 2 * head_dim), "ctx", axis=1, tiled=True
    )
    slot_queries = query_rot.reshape(slots_here, local_len, head_count, head_dim)

    def slot_forward(inputs):
        query_slot, kv_slot, pos_query, pos_key, length, order_row = inputs
        return attention_forward(query_slot, kv_slot, pos_query, pos_key, length)

    attention, log_total = lax.map(
        slot_forward, (slot_queries, slot_kv, query_pos, key_pos, lengths, block_order)
    )
    attention = attention.reshape(local_rows, head_count * head_dim)
    attn_low = attention.astype(jnp.bfloat16)
    residual = tokens_flat + jnp.dot(attn_low, out_full, preferred_element_type=jnp.float32)
    inverse_two = lax.rsqrt(jnp.mean(residual * residual, axis=1, keepdims=True) + EPSILON)
    unit_two = residual * inverse_two
    normed_ffn = (unit_two * gain_two.astype(jnp.float32)).astype(jnp.bfloat16)
    grad_out = jnp.where(
        live_rows, cotangent.reshape(local_rows, model_dim), jnp.zeros((), jnp.bfloat16)
    )
    gate_full, up_full, down_full = (
        lax.all_gather(w_gate, "fsdp", axis=1, tiled=True),
        lax.all_gather(w_up, "fsdp", axis=1, tiled=True),
        lax.all_gather(w_down, "fsdp", axis=1, tiled=True),
    )
    gate_proj = jnp.dot(normed_ffn, gate_full, preferred_element_type=jnp.float32)
    up_proj = jnp.dot(normed_ffn, up_full, preferred_element_type=jnp.float32)
    hidden = (jax.nn.silu(gate_proj) * up_proj).astype(jnp.bfloat16)
    ffn_out = contract_cols(hidden, down_full)
    grad_hidden = jnp.dot(grad_out, down_full, preferred_element_type=jnp.float32).astype(
        jnp.bfloat16
    )
    grad_gate, grad_up = swiglu_back(gate_proj, up_proj, grad_hidden)
    grad_normed = contract_cols(grad_gate, gate_full) + contract_cols(grad_up, up_full)
    ffn_grads = (
        lax.psum_scatter(
            split_term(normed_ffn, grad_gate, ctx_count, fsdp_count),
            ("ctx", "fsdp"),
            scatter_dimension=0,
            tiled=True,
        ),
        lax.psum_scatter(
            split_term(normed_ffn, grad_up, ctx_count, fsdp_count),
            ("ctx", "fsdp"),
            scatter_dimension=0,
            tiled=True,
        ),
        lax.psum_scatter(
            split_term(grad_out, hidden, ctx_count, fsdp_count),
            ("ctx", "fsdp"),
            scatter_dimension=0,
            tiled=True,
        ),
    )
    output = jnp.where(live_rows, residual + ffn_out, 0.0)
    grad_gain_two = jnp.sum(grad_normed * unit_two, axis=0)
    scaled_two = grad_normed * gain_two.astype(jnp.float32)
    grad_residual = grad_out.astype(jnp.float32) + inverse_two * (
        scaled_two - unit_two * jnp.mean(scaled_two * unit_two, axis=1, keepdims=True)
    )
    grad_branch = grad_residual.astype(jnp.bfloat16)
    grad_attn = contract_cols(grad_branch, out_full).astype(jnp.bfloat16)
    row_delta = jnp.sum(
        grad_attn.astype(jnp.float32).reshape(local_rows, head_count, head_dim)
        * attention.reshape(local_rows, head_count, head_dim),
        axis=2,
    )

    def slot_backward(inputs):
        (
            query_slot,
            kv_slot,
            pos_query,
            pos_key,
            length,
            log_slot,
            grad_slot,
            delta_slot,
            order_row,
        ) = inputs
        grad_query_slot, key_grads = attention_backward(
            query_slot, kv_slot, pos_query, pos_key, length, log_slot, grad_slot, delta_slot
        )
        return (grad_query_slot, key_grads)

    grad_query_rot, key_terms = lax.map(
        slot_backward,
        (
            slot_queries,
            slot_kv,
            query_pos,
            key_pos,
            lengths,
            log_total,
            grad_attn.reshape(slots_here, local_len, head_count, head_dim),
            row_delta.reshape(slots_here, local_len * head_count),
            block_order,
        ),
    )
    key_sums = lax.psum_scatter(
        key_terms.astype(jnp.bfloat16), "ctx", scatter_dimension=1, tiled=True
    ).astype(jnp.float32)
    kv_total = key_sums + jnp.where(
        live_rows.reshape(slots_here, local_len, 1), kv_cotangent.astype(jnp.float32), 0.0
    )
    grad_kv_low = kv_total.reshape(local_rows, 2 * head_dim).astype(jnp.bfloat16)
    grad_key = rotate(grad_kv_low[:, :head_dim].astype(jnp.float32), cosine, -sine_vals)
    grad_kv = jnp.concatenate(
        [grad_key, grad_kv_low[:, head_dim:].astype(jnp.float32)], axis=1
    ).astype(jnp.bfloat16)
    grad_qrot = (
        grad_query_rot.reshape(local_rows, head_count, head_dim)
        .astype(jnp.bfloat16)
        .astype(jnp.float32)
    )
    grad_query = (
        (rotate(grad_qrot, cosine[:, None, :], -sine_vals[:, None, :]) * head_dim ** (-0.5))
        .reshape(local_rows, head_count * head_dim)
        .astype(jnp.bfloat16)
    )
    grad_normed_one = contract_cols(grad_query, query_full) + contract_cols(grad_kv, kv_full)
    grad_gain_one = jnp.sum(grad_normed_one * unit_one, axis=0)
    scaled_one = grad_normed_one * gain_one.astype(jnp.float32)
    grad_tokens = grad_residual + inverse_one * (
        scaled_one - unit_one * jnp.mean(scaled_one * unit_one, axis=1, keepdims=True)
    )
    attn_grads = (
        lax.psum_scatter(
            contract_rows(normed_attn, grad_query), ("ctx", "fsdp"), scatter_dimension=0, tiled=True
        ),
        lax.psum_scatter(
            contract_rows(normed_attn, grad_kv), ("ctx", "fsdp"), scatter_dimension=0, tiled=True
        ),
        lax.psum_scatter(
            contract_rows(attn_low, grad_branch), ("ctx", "fsdp"), scatter_dimension=0, tiled=True
        ),
        lax.psum_scatter(grad_gain_one, ("ctx", "fsdp"), scatter_dimension=0, tiled=True),
        lax.psum_scatter(grad_gain_two, ("ctx", "fsdp"), scatter_dimension=0, tiled=True),
    )
    return (
        output.reshape(tokens.shape).astype(jnp.bfloat16),
        grad_tokens.reshape(tokens.shape).astype(jnp.bfloat16),
        attn_grads[0],
        attn_grads[1],
        attn_grads[2],
        attn_grads[3],
        attn_grads[4],
        ffn_grads[0],
        ffn_grads[1],
        ffn_grads[2],
    )


def solution(mesh):
    return jax.shard_map(
        shards,
        mesh=mesh,
        in_specs=(
            P("fsdp", "ctx", None),
            P("fsdp", "ctx", None),
            P("fsdp", "ctx", None),
            P("fsdp"),
            P("fsdp", None),
            P("fsdp", None),
            P("fsdp", None),
            P("fsdp", None),
            P("fsdp"),
            P("fsdp"),
            P(None, "fsdp"),
            P(None, "fsdp"),
            P(None, "fsdp"),
        ),
        out_specs=(
            P("fsdp", "ctx", None),
            P("fsdp", "ctx", None),
            P(("ctx", "fsdp"), None),
            P(("ctx", "fsdp"), None),
            P(("ctx", "fsdp"), None),
            P(("ctx", "fsdp")),
            P(("ctx", "fsdp")),
            P("ctx", "fsdp"),
            P("ctx", "fsdp"),
            P("ctx", "fsdp"),
        ),
        check_vma=False,
    )
```

profile of v0, /device:TPU:0, one launch (start us, length us, event | category | flops | bytes accessed | tf_op | source)
XLA Modules:
  0.0 5840.0 jit_solution(3675595155620998251)
XLA Ops:
  75.9 147.6 %all-gather.13.cloned.1.call-done = bf16[2048,2048]{1,0:T(8,128)(2,1)} async-done(((bf16[512,2048]{1,0:T(8,128)(2,1)}), bf16[2048,2048]{1,0:T(8,128)(2,1)}) %all-gather.13.cloned.1.call-update) | async-done | bytes 8388624 | tf_op jit(solution)/shard_map/all_gather | solution.py:189
  258.7 154.5 %while.58 = (s32[]{:T(128)}, f32[8192]{0:T(1024)S(1)}, f32[8192]{0:T(1024)S(1)}, s32[8]{0:T(128)S(1)}, s32[4096]{0:T(1024)S(1)}, /*index=5*/s32[]{:T(128)}, bf16...) while((s32[]{:T(128)}, f32[8192]{0:T(1024)S(1)}, ...), condition=%wide.region_4.5_spmd.clone, body=%wide.region_1.4_spmd.clone.sunk | while | flops 1111532032 | bytes 36384468 | solution.py:78
  413.8 110.5 %while.59 = (s32[]{:T(128)}, f32[8192,128]{1,0:T(8,128)}, s32[8]{0:T(128)S(1)}, s32[4096]{0:T(1024)S(1)}, s32[]{:T(128)}, /*index=5*/bf16[4096,128]{1,0:T(8,128)...) while((s32[]{:T(128)}, f32[8192,128]{1,0:T(8,128)}, ...), condition=%wide.region_6.7_spmd.clone, body=%wide.region_5.6_spmd.clone.sunk | while | flops 2170552832 | bytes 10922712 | solution.py:94
  546.5 217.1 %all-gather.17.cloned.1.call-done = bf16[2048,5632]{1,0:T(8,128)(2,1)} async-done(((bf16[2048,1408]{1,0:T(8,128)(2,1)}), bf16[2048,5632]{1,0:T(8,128)(2,1)}) %all-gather.17.cloned.1.call-update) | async-done | bytes 23068688 | tf_op jit(solution)/shard_map/all_gather | solution.py:231
  763.6 19.9 fusion.102
  783.5 371.0 %all-gather.21.cloned.1.call-done = bf16[2048,5632]{1,0:T(8,128)(2,1)} async-done(((bf16[2048,1408]{1,0:T(8,128)(2,1)}), bf16[2048,5632]{1,0:T(8,128)(2,1)}) %all-gather.21.cloned.1.call-update) | async-done | bytes 23068688 | tf_op jit(solution)/shard_map/all_gather | solution.py:233
  1172.9 372.6 %all-gather.19.cloned.1.call-done = bf16[2048,5632]{1,0:T(8,128)(2,1)} async-done(((bf16[2048,1408]{1,0:T(8,128)(2,1)}), bf16[2048,5632]{1,0:T(8,128)(2,1)}) %all-gather.19.cloned.1.call-update) | async-done | bytes 23068688 | tf_op jit(solution)/shard_map/all_gather | solution.py:232
  1545.5 27.0 fusion.34
  1572.6 19.5 fusion.103
  1632.9 354.3 %while.60 = (s32[]{:T(128)}, f32[8192,128]{1,0:T(8,128)}, bf16[8,512,256]{1,2,0:T(8,128)(2,1)}, s32[8]{0:T(128)S(1)}, s32[4096]{0:T(1024)}, /*index=5*/s32[]{:T(...) while((s32[]{:T(128)}, f32[8192,128]{1,0:T(8,128)}, ...), condition=%wide.region_11.12_spmd.clone, body=%wide.region_10.11_spmd.clone.sunk | while | flops 5404885504 | bytes 127214928 | solution.py:131
  1996.4 39.1 reduce-scatter.8.cloned.1.call-done
  2095.6 20.8 convolution_bitcast_fusion.2
  2116.4 33.3 copy.72
  2161.0 20.9 convolution_bitcast_fusion.1
  2181.9 33.5 copy.75
  2232.5 20.8 convolution_bitcast_fusion
  2253.3 33.3 copy.78
  2286.6 19.9 fusion.59
  2318.5 42.5 all-reduce.2
  2368.1 175.8 %reduce-scatter.14.cloned.1.call-done = f32[64,2048]{1,0:T(8,128)} async-done(((f32[2048,2048]{1,0:T(8,128)}), f32[64,2048]{1,0:T(8,128)}) %reduce-scatter.14.cloned.1.call-update) | async-done | bytes 524304 | tf_op jit(solution)/shard_map/reduce_scatter | solution.py:343
  2543.9 365.1 %reduce-scatter.10.cloned.1.call-done = f32[64,2048]{1,0:T(8,128)} async-done(((f32[2048,2048]{1,0:T(8,128)}), f32[64,2048]{1,0:T(8,128)}) %reduce-scatter.10.cloned.1.call-update) | async-done | bytes 524304 | tf_op jit(solution)/shard_map/reduce_scatter | solution.py:337
  2909.0 973.1 %reduce-scatter.16.cloned.1.call-done = f32[256,1408]{1,0:T(8,128)} async-done(((f32[8192,1408]{1,0:T(8,128)}), f32[256,1408]{1,0:T(8,128)}) %reduce-scatter.16.cloned.1.call-update) | async-done | bytes 1441808 | tf_op jit(solution)/shard_map/reduce_scatter | solution.py:245
  3882.1 975.7 %reduce-scatter.18.cloned.1.call-done = f32[256,1408]{1,0:T(8,128)} async-done(((f32[8192,1408]{1,0:T(8,128)}), f32[256,1408]{1,0:T(8,128)}) %reduce-scatter.18.cloned.1.call-update) | async-done | bytes 1441808 | tf_op jit(solution)/shard_map/reduce_scatter | solution.py:251
  4857.7 975.5 %reduce-scatter.20.cloned.1.call-done = f32[256,1408]{1,0:T(8,128)} async-done(((f32[8192,1408]{1,0:T(8,128)}), f32[256,1408]{1,0:T(8,128)}) %reduce-scatter.20.cloned.1.call-update) | async-done | bytes 1441808 | tf_op jit(solution)/shard_map/reduce_scatter | solution.py:257
  (446 shorter events, 903.0 us)
Async XLA Ops:
  7.2 33.1 all-gather.11.cloned.1.call-start
  7.9 64.3 %all-gather.23.cloned.1.call-start = ((), (), s32[]{:S(2)}) async-start(), calls=%async_computation.20 | async-start | bytes 2359296 | tf_op jit(solution)/shard_map/all_gather | solution.py:209
  22.2 213.9 %copy-start.28 = (f32[4,1,512]{2,1,0:T(1,128)}, f32[4,1,512]{2,1,0:T(1,128)S(1)}, u32[]{:S(2)}) copy-start(f32[4,1,512]{2,1,0:T(1,128)S(1)} %convert_element_type.188) | copy-start | bytes 24580
  26.3 209.9 %copy-start.34 = (f32[512]{0:T(512)}, f32[512]{0:T(512)S(1)}, u32[]{:S(2)}) copy-start(f32[512]{0:T(512)S(1)} %add_rsqrt_fusion.1) | copy-start | bytes 6148
  43.6 199.7 %copy-start.15 = (f32[512,64]{0,1:T(8,128)}, f32[512,64]{0,1:T(8,128)S(1)}, u32[]{:S(2)}) copy-start(f32[512,64]{0,1:T(8,128)S(1)} %get-tuple-element.548) | copy-start | bytes 393220
  44.4 179.1 %all-gather.13.cloned.1.call-start = ((), (), s32[]{:S(2)}) async-start(), calls=%async_computation.8 | async-start | bytes 10485760 | tf_op jit(solution)/shard_map/all_gather | solution.py:189
  45.1 488.2 %all-gather.15.cloned.1.call-start = ((), (), s32[]{:S(2)}) async-start(), calls=%async_computation.9 | async-start | bytes 10485760 | tf_op jit(solution)/shard_map/all_gather | solution.py:191
  45.7 717.9 %all-gather.17.cloned.1.call-start = ((), (), s32[]{:S(2)}) async-start(), calls=%async_computation.10 | async-start | bytes 28835840 | tf_op jit(solution)/shard_map/all_gather | solution.py:231
  46.3 1108.2 %all-gather.21.cloned.1.call-start = ((), (), s32[]{:S(2)}) async-start(), calls=%async_computation.12 | async-start | bytes 28835840 | tf_op jit(solution)/shard_map/all_gather | solution.py:233
  46.9 1498.6 %all-gather.19.cloned.1.call-start = ((), (), s32[]{:S(2)}) async-start(), calls=%async_computation.11 | async-start | bytes 28835840 | tf_op jit(solution)/shard_map/all_gather | solution.py:232
  47.6 1987.9 %reduce-scatter.8.cloned.1.call-start = ((), (), s32[]{:S(2)}) async-start(), calls=%async_computation.13 | async-start | bytes 2359296 | tf_op jit(solution)/shard_map/reduce_scatter | solution.py:309
  546.5 608.0 %copy-start.9 = (bf16[1,512,2048]{2,1,0:T(8,128)(2,1)S(1)}, bf16[1,512,2048]{2,1,0:T(8,128)(2,1)}, u32[]{:S(2)}) copy-start(bf16[1,512,2048]{2,1,0:T(8,128)(2,1)} %param.20) | copy-start | bytes 6291460
  546.5 608.0 %copy-start.37 = (pred[512]{0:T(512)(128)(4,1)S(1)}, pred[512]{0:T(512)(128)(4,1)}, u32[]{:S(2)}) copy-start(pred[512]{0:T(512)(128)(4,1)} %get-tuple-element.526) | copy-start | bytes 1540
  1991.4 45.2 copy-start.33
  1991.4 45.2 copy-start.42
  1991.4 45.8 copy-start.3
  1991.4 45.8 copy-start.29
  1991.4 45.8 copy-start.35
  1995.8 372.3 %reduce-scatter.12.cloned.1.call-start = ((), (), s32[]{:S(2)}) async-start(), calls=%async_computation.15 | async-start | bytes 2162688 | tf_op jit(solution)/shard_map/reduce_scatter | solution.py:340
  2039.7 504.2 %reduce-scatter.14.cloned.1.call-start = ((), (), s32[]{:S(2)}) async-start(), calls=%async_computation.16 | async-start | bytes 17301504 | tf_op jit(solution)/shard_map/reduce_scatter | solution.py:343
  2053.0 856.0 %reduce-scatter.10.cloned.1.call-start = ((), (), s32[]{:S(2)}) async-start(), calls=%async_computation.14 | async-start | bytes 17301504 | tf_op jit(solution)/shard_map/reduce_scatter | solution.py:337
  2080.3 1801.7 %reduce-scatter.16.cloned.1.call-start = ((), (), s32[]{:S(2)}) async-start(), calls=%async_computation.17 | async-start | bytes 47579136 | tf_op jit(solution)/shard_map/reduce_scatter | solution.py:245
  2149.7 2708.0 %reduce-scatter.18.cloned.1.call-start = ((), (), s32[]{:S(2)}) async-start(), calls=%async_computation.18 | async-start | bytes 47579136 | tf_op jit(solution)/shard_map/reduce_scatter | solution.py:251
  2215.4 3617.9 %reduce-scatter.20.cloned.1.call-start = ((), (), s32[]{:S(2)}) async-start(), calls=%async_computation.19 | async-start | bytes 47579136 | tf_op jit(solution)/shard_map/reduce_scatter | solution.py:257
  (57 other events, 538.3 us)
Sparse Core Ops, SparseCore 0:
  9.6 30.6 all-gather.10
  44.5 27.6 all-gather.22
  73.8 149.6 all-gather.12
  224.9 147.8 all-gather.14
  374.3 389.3 all-gather.16
  765.1 389.3 all-gather.20
  1156.1 389.3 all-gather.18
  1995.9 39.5 reduce-scatter.7
  2039.8 138.2 reduce-scatter.11
  2180.8 363.0 reduce-scatter.13
  2546.8 362.1 reduce-scatter.9
  2911.7 970.2 reduce-scatter.15
  3884.9 972.7 reduce-scatter.17
  4860.5 972.7 reduce-scatter.19
where the time goes:
time: 5850 us; the launch traced here: 5840 us
  waiting for transfers between devices  4640 us (79%)
  matrix products  733 us (13%)
  local copies, waits for them, and re-layouts  224 us (4%)
  other arithmetic  138 us (2%)
  blocking collectives  68.2 us (1%)
    reduce_scatter x1, waiting for transfers between devices, shards(): lax.psum_scatter(split_term(normed_ffn, grad_up, ctx_count, fsdp_count),...  976 us
    reduce_scatter x1, waiting for transfers between devices, shards(): lax.psum_scatter(split_term(grad_out, hidden, ctx_count, fsdp_count), ('c...  976 us
    reduce_scatter x1, waiting for transfers between devices, shards(): lax.psum_scatter(split_term(normed_ffn, grad_gate, ctx_count, fsdp_count)...  973 us
    all_gather x1, waiting for transfers between devices, shards(): lax.all_gather(w_up, 'fsdp', axis=1, tiled=True)  373 us
    all_gather x1, waiting for transfers between devices, shards(): lax.all_gather(w_down, 'fsdp', axis=1, tiled=True)  371 us
    reduce_scatter x1, waiting for transfers between devices, shards(): lax.psum_scatter(contract_rows(normed_attn, grad_query), ('ctx', 'fsdp'),...  365 us
    dot_general x30, matrix products, contract_cols(): lax.dot_general(left, right, (((1,), (1,)), ((), ())), preferred_element_...  304 us
    all_gather x1, waiting for transfers between devices, shards(): lax.all_gather(w_gate, 'fsdp', axis=1, tiled=True)  217 us
  transfers between devices with their start and end apart: 14, of which 12 were waited for; matrix products, arithmetic and copies ran while one was open for 11% of the time, Pallas kernels for 0%

commit v1 on v0

--- a/solution.py
+++ b/solution.py
@@ -1,3 +1,4 @@
+import functools
 import jax
 import jax.numpy as jnp
 from jax import lax
@@ -8,6 +9,37 @@
 EPSILON = 1e-05
 ROPE_BASE = 10000.0
 MASKED = -1e30
+
+
+def store_skins_by_axis(chunk, dim_i):
+    tmp = list(chunk.shape[1:])
+    tmp[dim_i] *= chunk.shape[0]
+    return jnp.moveaxis(chunk, 0, dim_i).reshape(tmp)
+
+
+def pass_tokens_now(state, a_name, d0):
+    degree = lax.axis_size(a_name)
+    pile = tuple(((j, (j + 1) % degree) for j in range(degree)))
+    base_arr, f_next = ([], [])
+    src_i = 0
+    inbox = tuple(((c, idx) for idx, c in pile))
+    while src_i < degree - 1:
+        if src_i % 2 == 0:
+            block_last = lax.ppermute(base_arr[-1] if base_arr else state, a_name, pile)
+            base_arr.append(block_last)
+        else:
+            f_now = lax.ppermute(f_next[-1] if f_next else state, a_name, inbox)
+            f_next.append(f_now)
+        src_i = src_i + 1
+    o_now = jnp.stack([*base_arr[::-1], state, *f_next], 0)
+    mid_arr = len(base_arr)
+    then = lax.axis_index(a_name)
+    long_array = then - mid_arr
+    o_now = o_now[(jnp.arange(degree) - long_array) % degree]
+    return store_skins_by_axis(o_now, d0)
+
+
+recover_the_shards = functools.partial(pass_tokens_now, a_name="fsdp", d0=1)
 
 
 def angles(positions, head_dim):
@@ -229,7 +261,7 @@
     )
     gate_full, up_full, down_full = (
         lax.all_gather(w_gate, "fsdp", axis=1, tiled=True),
-        lax.all_gather(w_up, "fsdp", axis=1, tiled=True),
+        recover_the_shards(w_up),
         lax.all_gather(w_down, "fsdp", axis=1, tiled=True),
     )
     gate_proj = jnp.dot(normed_ffn, gate_full, preferred_element_type=jnp.float32)

time: 5850 us -> 5790 us (0.990)
  waiting for transfers between devices: 4640 us -> 4020 us
  blocking collectives: 68.2 us -> 418 us
  local copies, waits for them, and re-layouts: 224 us -> 339 us
  starting transfers between devices: 1.13 us -> 108 us
    all_gather x1 -> x0, waiting for transfers between devices: 373 us -> none  [shards(): lax.all_gather(w_up, 'fsdp', axis=1, tiled=True)]
    all_gather x1, blocking collectives: 12.2 us -> 360 us  [shards(): lax.all_gather(gain_ffn, 'fsdp', axis=0, tiled=True)]
    all_gather x1, waiting for transfers between devices: 217 us -> 0.01 us  [shards(): lax.all_gather(w_gate, 'fsdp', axis=1, tiled=True)]
    ppermute x0 -> x3, waiting for transfers between devices: none -> 213 us  [the longest x2 213 us: pass_tokens_now(): block_last = lax.ppermute(base_arr[-1] if base_arr else state, a_name, pile)]
    all_gather x1, waiting for transfers between devices: 148 us -> 0.01 us  [shards(): lax.all_gather(w_query, 'fsdp', axis=0, tiled=True)]
    ppermute x0 -> x3, starting transfers between devices: none -> 108 us  [the longest x2 106 us: pass_tokens_now(): block_last = lax.ppermute(base_arr[-1] if base_arr else state, a_name, pile)]
    gather x0 -> x35, local copies, waits for them, and re-layouts: none -> 95.3 us
    all_gather x1, waiting for transfers between devices: 371 us -> 288 us  [shards(): lax.all_gather(w_down, 'fsdp', axis=1, tiled=True)]
  transfers between devices with their start and end apart: 14 -> 16, of which waited for: 12 -> 9; matrix products, arithmetic and copies ran while one was open for 11% -> 12% of each run, Pallas kernels for 0% -> 0%
where the time goes in v1:
time: 5790 us; the launch traced here: 5780 us
  waiting for transfers between devices  4020 us (69%)
  matrix products  710 us (12%)
  blocking collectives  418 us (7%)
  local copies, waits for them, and re-layouts  339 us (6%)
  other arithmetic  153 us (3%)
  starting transfers between devices  108 us (2%)
    reduce_scatter x1, waiting for transfers between devices, shards(): lax.psum_scatter(split_term(normed_ffn, grad_up, ctx_count, fsdp_count),...  976 us
    reduce_scatter x1, waiting for transfers between devices, shards(): lax.psum_scatter(split_term(normed_ffn, grad_gate, ctx_count, fsdp_count)...  976 us
    reduce_scatter x1, waiting for transfers between devices, shards(): lax.psum_scatter(split_term(grad_out, hidden, ctx_count, fsdp_count), ('c...  973 us
    reduce_scatter x1, waiting for transfers between devices, shards(): lax.psum_scatter(contract_rows(normed_attn, grad_query), ('ctx', 'fsdp'),...  365 us
    all_gather x1, blocking collectives, shards(): lax.all_gather(gain_ffn, 'fsdp', axis=0, tiled=True)  360 us
    all_gather x1, waiting for transfers between devices, shards(): lax.all_gather(w_down, 'fsdp', axis=1, tiled=True)  288 us
    dot_general x30, matrix products, contract_cols(): lax.dot_general(left, right, (((1,), (1,)), ((), ())), preferred_element_...  283 us
    ppermute x2, waiting for transfers between devices, pass_tokens_now(): block_last = lax.ppermute(base_arr[-1] if base_arr else state, a_name, pile)  213 us
  transfers between devices with their start and end apart: 16, of which 9 were waited for; matrix products, arithmetic and copies ran while one was open for 12% of the time, Pallas kernels for 0%

profile of v1, /device:TPU:0, one launch (start us, length us, event | category | flops | bytes accessed | tf_op | source)
XLA Modules:
  0.0 5781.5 jit_solution(17441122073462700453)
XLA Ops:
  50.2 213.1 %collective-permute-done = bf16[2048,1408]{1,0:T(8,128)(2,1)} collective-permute-done((bf16[2048,1408]{1,0:T(8,128)(2,1)}, bf16[2048,1408]{1,0:T(8,128)(2,1)}, u32[]{:S(2)}, u32[]{:S(2)}) %collective-permute-start) | collective-permute-done | bytes 5767200 | tf_op jit(solution)/shard_map/ppermute | solution.py:28
  263.4 104.0 %collective-permute-start.1 = (bf16[2048,1408]{1,0:T(8,128)(2,1)}, bf16[2048,1408]{1,0:T(8,128)(2,1)}, u32[]{:S(2)}, u32[]{:S(2)}) collective-permute-start(bf16[2048,1408]{1,0:T(8,128)(2,1)} %collective-permute-done), channel_id=1, source_target_pairs={{0,1},{1,2},{2,3},{3,0},{4,5},{5,6},{6,7},{7,4},{8,9},{9,10},{10,1... | collective-permute-start | bytes 17301512 | tf_op jit(solution)/shard_map/ppermute | solution.py:28
  367.5 360.4 %all-gather.2 = bf16[4,1,512]{2,1,0:T(2,128)(2,1)S(1)} all-gather(bf16[1,1,512]{2,1,0:T(2,128)(2,1)S(1)} %reshape.479), channel_id=1, replica_groups=mesh['ctx'=8,'fsdp'=4] {'fsdp'}, dimensions={0}, use_global_device_ids=true | all-gather | bytes 5120 | tf_op jit(solution)/shard_map/all_gather | solution.py:225
  788.0 34.5 while.61
  826.5 34.5 while.60
  911.7 101.8 %while.62 = (s32[]{:T(128)}, f32[8192]{0:T(1024)S(1)}, f32[8192]{0:T(1024)S(1)}, s32[8]{0:T(128)S(1)}, s32[4096]{0:T(1024)S(1)}, /*index=5*/s32[]{:T(128)}, bf16...) while((s32[]{:T(128)}, f32[8192]{0:T(1024)S(1)}, ...), condition=%wide.region_4.5_spmd.clone, body=%wide.region_1.4_spmd.clone.sunk | while | flops 1111532032 | bytes 36384468 | solution.py:110
  1013.5 111.1 %while.63 = (s32[]{:T(128)}, f32[8192,128]{1,0:T(8,128)}, s32[8]{0:T(128)S(1)}, s32[4096]{0:T(1024)S(1)}, s32[]{:T(128)}, /*index=5*/bf16[4096,128]{1,0:T(8,128)...) while((s32[]{:T(128)}, f32[8192,128]{1,0:T(8,128)}, ...), condition=%wide.region_6.7_spmd.clone, body=%wide.region_5.6_spmd.clone.sunk | while | flops 2170552832 | bytes 10922712 | solution.py:126
  1166.5 287.9 %all-gather.18.cloned.1.call-done = bf16[2048,5632]{1,0:T(8,128)(2,1)} async-done(((bf16[2048,1408]{1,0:T(8,128)(2,1)}), bf16[2048,5632]{1,0:T(8,128)(2,1)}) %all-gather.18.cloned.1.call-update) | async-done | bytes 23068688 | tf_op jit(solution)/shard_map/all_gather | solution.py:265
  1472.7 27.1 fusion.34
  1519.3 22.8 multiply_reduce_fusion
  1565.0 363.7 %while.64 = (s32[]{:T(128)}, f32[8192,128]{1,0:T(8,128)}, bf16[8,512,256]{1,2,0:T(8,128)(2,1)}, s32[8]{0:T(128)S(1)}, s32[4096]{0:T(1024)}, /*index=5*/s32[]{:T(...) while((s32[]{:T(128)}, f32[8192,128]{1,0:T(8,128)}, ...), condition=%wide.region_11.12_spmd.clone, body=%wide.region_10.11_spmd.clone.sunk | while | flops 5404885504 | bytes 160769360 | solution.py:163
  1937.4 39.5 reduce-scatter.8.cloned.1.call-done
  2039.1 20.8 convolution_bitcast_fusion
  2059.9 33.4 copy.107
  2108.6 21.0 convolution_bitcast_fusion.2
  2129.5 33.4 copy.101
  2174.3 21.0 convolution_bitcast_fusion.1
  2195.2 33.5 copy.104
  2261.3 43.8 all-reduce.2
  2312.2 173.1 %reduce-scatter.14.cloned.1.call-done = f32[64,2048]{1,0:T(8,128)} async-done(((f32[2048,2048]{1,0:T(8,128)}), f32[64,2048]{1,0:T(8,128)}) %reduce-scatter.14.cloned.1.call-update) | async-done | bytes 524304 | tf_op jit(solution)/shard_map/reduce_scatter | solution.py:375
  2485.4 364.9 %reduce-scatter.10.cloned.1.call-done = f32[64,2048]{1,0:T(8,128)} async-done(((f32[2048,2048]{1,0:T(8,128)}), f32[64,2048]{1,0:T(8,128)}) %reduce-scatter.10.cloned.1.call-update) | async-done | bytes 524304 | tf_op jit(solution)/shard_map/reduce_scatter | solution.py:369
  2850.3 973.2 %reduce-scatter.20.cloned.1.call-done = f32[256,1408]{1,0:T(8,128)} async-done(((f32[8192,1408]{1,0:T(8,128)}), f32[256,1408]{1,0:T(8,128)}) %reduce-scatter.20.cloned.1.call-update) | async-done | bytes 1441808 | tf_op jit(solution)/shard_map/reduce_scatter | solution.py:289
  3823.5 975.5 %reduce-scatter.16.cloned.1.call-done = f32[256,1408]{1,0:T(8,128)} async-done(((f32[8192,1408]{1,0:T(8,128)}), f32[256,1408]{1,0:T(8,128)}) %reduce-scatter.16.cloned.1.call-update) | async-done | bytes 1441808 | tf_op jit(solution)/shard_map/reduce_scatter | solution.py:277
  4799.0 975.7 %reduce-scatter.18.cloned.1.call-done = f32[256,1408]{1,0:T(8,128)} async-done(((f32[8192,1408]{1,0:T(8,128)}), f32[256,1408]{1,0:T(8,128)}) %reduce-scatter.18.cloned.1.call-update) | async-done | bytes 1441808 | tf_op jit(solution)/shard_map/reduce_scatter | solution.py:283
  (493 shorter events, 1024.1 us)
Async XLA Ops:
  7.2 33.1 all-gather.10.cloned.1.call-start
  7.9 720.7 %all-gather.20.cloned.1.call-start = ((), (), s32[]{:S(2)}) async-start(), calls=%async_computation.19 | async-start | bytes 2359296 | tf_op jit(solution)/shard_map/all_gather | solution.py:241
  22.8 866.3 %copy-start.30 = (f32[4,1,512]{2,1,0:T(1,128)}, f32[4,1,512]{2,1,0:T(1,128)S(1)}, u32[]{:S(2)}) copy-start(f32[4,1,512]{2,1,0:T(1,128)S(1)} %convert_element_type.188) | copy-start | bytes 24580
  26.3 862.8 %copy-start.37 = (f32[512]{0:T(512)}, f32[512]{0:T(512)S(1)}, u32[]{:S(2)}) copy-start(f32[512]{0:T(512)S(1)} %add_rsqrt_fusion.1) | copy-start | bytes 6148
  43.6 852.7 %copy-start.16 = (f32[512,64]{0,1:T(8,128)}, f32[512,64]{0,1:T(8,128)S(1)}, u32[]{:S(2)}) copy-start(f32[512,64]{0,1:T(8,128)S(1)} %get-tuple-element.614) | copy-start | bytes 393220
  44.4 832.5 %all-gather.12.cloned.1.call-start = ((), (), s32[]{:S(2)}) async-start(), calls=%async_computation.8 | async-start | bytes 10485760 | tf_op jit(solution)/shard_map/all_gather | solution.py:221
  45.1 1088.1 %all-gather.14.cloned.1.call-start = ((), (), s32[]{:S(2)}) async-start(), calls=%async_computation.9 | async-start | bytes 10485760 | tf_op jit(solution)/shard_map/all_gather | solution.py:223
  45.7 1100.7 %all-gather.16.cloned.1.call-start = ((), (), s32[]{:S(2)}) async-start(), calls=%async_computation.10 | async-start | bytes 28835840 | tf_op jit(solution)/shard_map/all_gather | solution.py:263
  46.3 321.2 %copy-start.46 = (bf16[512]{0:T(512)(128)(2,1)S(1)}, bf16[512]{0:T(512)(128)(2,1)}, u32[]{:S(2)}) copy-start(bf16[512]{0:T(512)(128)(2,1)} %param.28) | copy-start | bytes 3076
  46.3 1408.0 %all-gather.18.cloned.1.call-start = ((), (), s32[]{:S(2)}) async-start(), calls=%async_computation.11 | async-start | bytes 28835840 | tf_op jit(solution)/shard_map/all_gather | solution.py:265
  46.4 217.0 %collective-permute-start = (bf16[2048,1408]{1,0:T(8,128)(2,1)}, bf16[2048,1408]{1,0:T(8,128)(2,1)}, u32[]{:S(2)}, u32[]{:S(2)}) collective-permute-start(bf16[2048,1408]{1,0:T(8,128)(2,1)} %param.30), channel_id=1, source_target_pairs={{0,1},{1,2},{2,3},{3,0},{4,5},{5,6},{6,7},{7,4},{8,9},{9,10},{10,1... | collective-permute-start | bytes 17301512 | tf_op jit(solution)/shard_map/ppermute | solution.py:28
  47.9 685.1 %collective-permute-start.2 = (bf16[2048,1408]{1,0:T(8,128)(2,1)}, bf16[2048,1408]{1,0:T(8,128)(2,1)}, u32[]{:S(2)}, u32[]{:S(2)}) collective-permute-start(bf16[2048,1408]{1,0:T(8,128)(2,1)} %param.30), channel_id=1, source_target_pairs={{1,0},{2,1},{3,2},{0,3},{5,4},{6,5},{7,6},{4,7},{9,8},{10,9},{11,1... | collective-permute-start | bytes 17301512 | tf_op jit(solution)/shard_map/ppermute | solution.py:31
  263.4 469.6 %collective-permute-start.1 = (bf16[2048,1408]{1,0:T(8,128)(2,1)}, bf16[2048,1408]{1,0:T(8,128)(2,1)}, u32[]{:S(2)}, u32[]{:S(2)}) collective-permute-start(bf16[2048,1408]{1,0:T(8,128)(2,1)} %collective-permute-done), channel_id=1, source_target_pairs={{0,1},{1,2},{2,3},{3,0},{4,5},{5,6},{6,7},{7,4},{8,9},{9,10},{10,1... | collective-permute-start | bytes 17301512 | tf_op jit(solution)/shard_map/ppermute | solution.py:28
  367.4 1609.5 %reduce-scatter.8.cloned.1.call-start = ((), (), s32[]{:S(2)}) async-start(), calls=%async_computation.12 | async-start | bytes 2359296 | tf_op jit(solution)/shard_map/reduce_scatter | solution.py:341
  1146.4 307.9 %copy-start.11 = (bf16[1,512,2048]{2,1,0:T(8,128)(2,1)S(1)}, bf16[1,512,2048]{2,1,0:T(8,128)(2,1)}, u32[]{:S(2)}) copy-start(bf16[1,512,2048]{2,1,0:T(8,128)(2,1)} %param.20) | copy-start | bytes 6291460
  1146.4 307.9 %copy-start.40 = (pred[512]{0:T(512)(128)(4,1)S(1)}, pred[512]{0:T(512)(128)(4,1)}, u32[]{:S(2)}) copy-start(pred[512]{0:T(512)(128)(4,1)} %get-tuple-element.590) | copy-start | bytes 1540
  1932.8 45.8 copy-start.5
  1932.8 45.8 copy-start.31
  1937.2 375.0 %reduce-scatter.12.cloned.1.call-start = ((), (), s32[]{:S(2)}) async-start(), calls=%async_computation.14 | async-start | bytes 2162688 | tf_op jit(solution)/shard_map/reduce_scatter | solution.py:372
  1981.0 504.3 %reduce-scatter.14.cloned.1.call-start = ((), (), s32[]{:S(2)}) async-start(), calls=%async_computation.15 | async-start | bytes 17301504 | tf_op jit(solution)/shard_map/reduce_scatter | solution.py:375
  1994.3 856.0 %reduce-scatter.10.cloned.1.call-start = ((), (), s32[]{:S(2)}) async-start(), calls=%async_computation.13 | async-start | bytes 17301504 | tf_op jit(solution)/shard_map/reduce_scatter | solution.py:369
  2022.1 1801.4 %reduce-scatter.20.cloned.1.call-start = ((), (), s32[]{:S(2)}) async-start(), calls=%async_computation.18 | async-start | bytes 47579136 | tf_op jit(solution)/shard_map/reduce_scatter | solution.py:289
  2093.3 2705.8 %reduce-scatter.16.cloned.1.call-start = ((), (), s32[]{:S(2)}) async-start(), calls=%async_computation.16 | async-start | bytes 47579136 | tf_op jit(solution)/shard_map/reduce_scatter | solution.py:277
  2162.9 3611.8 %reduce-scatter.18.cloned.1.call-start = ((), (), s32[]{:S(2)}) async-start(), calls=%async_computation.17 | async-start | bytes 47579136 | tf_op jit(solution)/shard_map/reduce_scatter | solution.py:283
  (62 other events, 617.6 us)
Sparse Core Ops, SparseCore 0:
  9.6 30.6 all-gather.9
  44.5 27.6 all-gather.19
  73.8 303.2 all-gather.11
  378.5 282.0 all-gather.13
  662.1 400.7 all-gather.15
  1064.4 389.9 all-gather.17
  1937.3 39.4 reduce-scatter.7
  1981.2 138.2 reduce-scatter.11
  2122.4 362.9 reduce-scatter.13
  2488.1 362.1 reduce-scatter.9
  2853.2 970.2 reduce-scatter.19
  3826.2 972.7 reduce-scatter.15
  4801.9 972.7 reduce-scatter.17
